TPU v7x, 32 devices: a whole 2x2x4 slice. The times are simulated.
32 devices in a mesh: batch: 2 (over y), seq: 16 (over z, x, core).
Axes of the slice: x: 2, y: 2, z: 4, core: 2. Of those that a mesh axis runs over, the one named last changes fastest.
Arguments:
- tokens: bfloat16 [32, 64, 32, 768], P('batch', None, 'seq'), may hold values from -6 to 6
- lengths: int32 [32], P('batch'), may hold values from 256 to 2048
- labels: int32 [32, 64, 32], P('batch', None, 'seq'), may hold values from 0 to 767
- picked: int32 [32, 64, 32], P('batch', None, 'seq'), may hold values 0 or 1
- cotangent: bfloat16 [32, 64, 32, 768], P('batch', None, 'seq'), may hold values from -6 to 6
- w_in: bfloat16 [1, 768, 3072], P(None, None, ('batch', 'seq')), may hold values from -0.21875 to 0.21875
- b_in: bfloat16 [1, 3072], P(None, ('batch', 'seq')), may hold values from -1.796875 to 1.796875
- w_out: bfloat16 [1, 3072, 768], P(None, ('batch', 'seq')), may hold values from -0.109375 to 0.109375
- shifts: bfloat16 [1, 3, 768], P(None, None, ('batch', 'seq')), may hold values from -1.796875 to 1.796875
- norm_gains: bfloat16 [1, 2, 768], P(None, None, ('batch', 'seq')), may hold values from 0.25 to 1.75
Outputs:
- mixed: bfloat16 [32, 64, 32, 768], P('batch', None, 'seq')
- input_grad: bfloat16 [32, 64, 32, 768], P('batch', None, 'seq')
- grad_w_in: float32 [1, 768, 3072], P(None, None, ('batch', 'seq'))
- grad_b_in: float32 [1, 3072], P(None, ('batch', 'seq'))
- grad_w_out: float32 [1, 3072, 768], P(None, ('batch', 'seq'))
- grad_shifts: float32 [1, 3, 768], P(None, None, ('batch', 'seq'))
- grad_gains: float32 [1, 2, 768], P(None, None, ('batch', 'seq'))
- match_rate: float32 [], replicated
All inputs are finite; a program needn't handle non-finite values. No bound on the sum of `picked` on one device may be relied on, other than what follows from the above.
Results may differ from a plain program's by a relative error of at most 0.0095.
Values may be sent and summed in bfloat16 or wider, within the bound.
No kernel may reach another device: no remote copies, remote signals or barrier semaphores. Data moves between devices by JAX's collectives and lax.ppermute only.
A program may use at most 192 MiB of HBM per device.

v0:
```python
import math
import jax
import jax.numpy as jnp
from jax import lax
from jax.sharding import PartitionSpec as P

D = 768
L1 = 64
L2 = 32
L = 2048
EPSILON = 1e-12
ROOT_TWO_PI = 0.7978845608028654
F32 = jnp.float32
BF16 = jnp.bfloat16


def layer_norm(values, gain_rows, shift_rows):
    center = values - jnp.mean(values, axis=-1, keepdims=True)
    spread = jnp.mean(center * center, axis=-1, keepdims=True)
    return center * lax.rsqrt(spread + EPSILON) * gain_rows + shift_rows


def gelu(values):
    return (
        0.5
        * values
        * (1.0 + jnp.tanh(ROOT_TWO_PI * (values + 0.044715 * values * values * values)))
    )


def table_pair(points):
    numbers = jnp.arange(points, dtype=jnp.int32)
    product_mod = numbers[:, None] * numbers[None, :] % points
    angles = product_mod.astype(F32) * (2.0 * math.pi / points)
    factor = 1.0 / math.sqrt(points)
    return ((jnp.cos(angles) * factor).astype(BF16), (jnp.sin(angles) * factor).astype(BF16))


def twiddles():
    row_index = jnp.arange(L1, dtype=jnp.int32)[None, :]
    col_index = jnp.arange(L2, dtype=jnp.int32)[:, None]
    angles = (row_index * col_index % L).astype(F32) * (2.0 * math.pi / L)
    return (jnp.cos(angles)[:, :, None], jnp.sin(angles)[:, :, None])


def swap(values, step):
    axis, mask = step
    size = lax.axis_size(axis)
    return lax.ppermute(values, axis, [(i, i ^ mask) for i in range(size)])


def bits(size):
    masks = []
    mask = size // 2
    while mask >= 1:
        masks.append(mask)
        mask //= 2
    return masks


def xor_gather(block, steps):
    held = block[None]
    for step in steps:
        held = jnp.concatenate([held, swap(held, step)], axis=0)
    return held


def xor_scatter(held, steps):
    for step in reversed(steps):
        half = held.shape[0] // 2
        arrived = swap(held[half:].astype(BF16), step)
        held = held[:half].astype(F32) + arrived.astype(F32)
    return held[0]


def body(tokens, lengths, labels, picked, cotangent, w_in, b_in, w_out, shifts, norm_gains):
    groups = lax.axis_size("seq")
    me = lax.axis_index("seq")
    columns = tokens.shape[2]
    share = w_in.shape[2]
    steps = (
        [("seq", mask) for mask in bits(groups)[:-1]]
        + [("batch", mask) for mask in bits(lax.axis_size("batch"))]
        + [("seq", 1)]
    )
    early = len(bits(groups)) - 1
    own = jnp.stack([w_in[0].T, w_out[0]])
    held = own[None]
    for step in steps[: early - 1]:
        held = jnp.concatenate([held, swap(held, step)], axis=0)
    tokens_late, held = lax.optimization_barrier((tokens, held))
    for step in steps[early - 1 :]:
        held = jnp.concatenate([held, swap(held, step)], axis=0)
    hidden_units = held.shape[0] * share
    w_first = held[:, 0].reshape(hidden_units, D)
    w_second = held[:, 1].reshape(hidden_units, D)
    packed = jnp.concatenate([shifts[0].reshape(-1), norm_gains[0].reshape(-1)])
    packed = lax.all_gather(packed, ("batch", "seq"), axis=0)
    rows = packed.reshape(packed.shape[0], 5, -1).transpose(1, 0, 2).reshape(5, D)
    shifts_f = rows[:3].astype(F32)
    gains_f = rows[3:].astype(F32)
    b_first = xor_gather(b_in[0].astype(F32), steps).reshape(hidden_units)
    short_cos, short_sin = table_pair(L1)
    long_cos, long_sin = table_pair(L2)
    wide_cos, wide_sin = table_pair(D)
    short_table = jnp.concatenate([short_cos, short_sin], axis=0)
    long_table = jnp.stack([jnp.stack([long_cos, -long_sin]), jnp.stack([long_sin, long_cos])])
    both = jnp.eye(2, dtype=BF16)
    pair_table = jnp.einsum("qukm,bc->qkbcum", long_table, both).reshape(4 * L2, 4 * L2)
    wide = jnp.stack([wide_cos, -wide_sin])
    twiddle_cos, twiddle_sin = twiddles()
    x_all = lax.all_to_all(tokens_late, "seq", split_axis=0, concat_axis=0, tiled=True)
    x_all, late_cotangent = lax.optimization_barrier((x_all, cotangent))
    g_all = lax.all_to_all(late_cotangent, "seq", split_axis=0, concat_axis=0, tiled=True)
    length = lengths[me]
    spots = L2 * jnp.arange(L1, dtype=jnp.int32)[None, :] + jnp.arange(L2, dtype=jnp.int32)[:, None]
    x_rows = x_all.transpose(0, 2, 1, 3).reshape(L2, L1, D)
    x_rows = jnp.where((spots < length)[:, :, None], x_rows, jnp.zeros_like(x_rows))
    first = jnp.einsum("kn,mnd->mkd", short_table, x_rows, preferred_element_type=F32)
    first_cos, first_sin = (first[:, :L1], first[:, L1:])
    turned_cos = (first_cos * twiddle_cos - first_sin * twiddle_sin).astype(BF16)
    turned_sin = (first_cos * twiddle_sin + first_sin * twiddle_cos).astype(BF16)
    turned = jnp.stack([turned_cos, turned_sin]).reshape(2, L2, 2, L2, D)
    turned = turned.transpose(3, 2, 0, 1, 4).reshape(L2, 4 * L2, D)
    spectrum = jnp.einsum("rk,lkd->lrd", pair_table, turned, preferred_element_type=F32)
    spectrum = spectrum.astype(BF16).reshape(L2, 2, L1, D)
    mixed = jnp.einsum("lund,ude->lne", spectrum, wide, preferred_element_type=F32)
    residual = (x_rows.astype(F32) + mixed).reshape(L, D)
    normed = layer_norm(residual, gains_f[0], shifts_f[1])
    normed_low = normed.astype(BF16)
    pre_act = jnp.einsum("td,fd->tf", normed_low, w_first, preferred_element_type=F32) + b_first
    act_low = gelu(pre_act).astype(BF16)
    summed = normed + jnp.dot(act_low, w_second, preferred_element_type=F32) + shifts_f[0]
    layer_out = layer_norm(summed, gains_f[1], shifts_f[2]).astype(BF16)
    out_rows = layer_out.reshape(groups, columns, L1, D)
    out_rows = lax.all_to_all(out_rows, "seq", split_axis=0, concat_axis=0, tiled=True)
    current = out_rows.transpose(0, 2, 1, 3)
    grad_out = g_all.transpose(0, 2, 1, 3).reshape(L, D).astype(F32)
    unused, pull_second = jax.vjp(layer_norm, summed, gains_f[1], shifts_f[2])
    grad_summed, grad_gain_two, grad_shift_two = pull_second(grad_out)
    grad_bias_two = jnp.sum(grad_summed, axis=0)
    summed_low = grad_summed.astype(BF16)
    grad_w_second = jnp.einsum("tf,td->fd", act_low, summed_low, preferred_element_type=F32)
    grad_act = jnp.einsum("td,fd->tf", summed_low, w_second, preferred_element_type=F32)
    unused_act, pull_gelu = jax.vjp(gelu, pre_act)
    grad_pre = pull_gelu(grad_act)[0]
    grad_b_first = jnp.sum(grad_pre, axis=0)
    pre_low = grad_pre.astype(BF16)
    grad_w_first = jnp.einsum("tf,td->fd", pre_low, normed_low, preferred_element_type=F32)
    grad_normed = grad_summed + jnp.dot(pre_low, w_first, preferred_element_type=F32)
    normed_again, pull_first = jax.vjp(layer_norm, residual, gains_f[0], shifts_f[1])
    grad_residual, grad_gain_one, grad_shift_one = pull_first(grad_normed)
    residual_low = grad_residual.astype(BF16).reshape(L2, L1, D)
    grad_spectrum = jnp.einsum("lne,ude->lund", residual_low, wide, preferred_element_type=F32)
    grad_spectrum = grad_spectrum.astype(BF16).reshape(L2, 4 * L2, D)
    grad_turned = jnp.einsum("rk,lrd->lkd", pair_table, grad_spectrum, preferred_element_type=F32)
    grad_turned = grad_turned.astype(BF16).reshape(L2, 2, 2, L2, D).transpose(2, 3, 1, 0, 4)
    grad_turned = grad_turned.reshape(2, L2, L1, D)
    grad_cos, grad_sin = (grad_turned[0], grad_turned[1])
    back_cos = grad_cos * twiddle_cos + grad_sin * twiddle_sin
    back_sin = grad_sin * twiddle_cos - grad_cos * twiddle_sin
    stacked = jnp.concatenate([back_cos, back_sin], axis=1).astype(BF16)
    grad_x = residual_low.astype(F32) + jnp.einsum(
        "kn,mkd->mnd", short_table, stacked, preferred_element_type=F32
    )
    grad_x = jnp.where((spots < length)[:, :, None], grad_x, 0.0).astype(BF16)
    grad_x = grad_x.reshape(groups, columns, L1, D)
    grad_x = lax.all_to_all(grad_x, "seq", split_axis=0, concat_axis=0, tiled=True)
    input_grad = grad_x.transpose(0, 2, 1, 3)
    grad_first = xor_scatter(grad_w_first.reshape(-1, share, D), steps)
    grad_second = xor_scatter(grad_w_second.reshape(-1, share, D), steps)
    hidden_total = hidden_units
    here = lax.axis_index("batch") * groups + me
    blocks = grad_b_first.reshape(-1, share)
    block_of = []
    for number in range(blocks.shape[0]):
        code_seq, code_batch = (0, 0)
        for place, (axis, mask) in enumerate(steps):
            if number >> place & 1:
                if axis == "seq":
                    code_seq ^= mask
                else:
                    code_batch ^= mask
        block_of.append(code_batch * groups + code_seq)
    owner = jnp.array(block_of, dtype=jnp.int32) ^ here
    one_hot = (owner[None, :] == jnp.arange(blocks.shape[0], dtype=jnp.int32)[:, None]).astype(F32)
    ordered = jnp.sum(one_hot[:, :, None] * blocks[None], axis=1).reshape(hidden_total // D, D)
    shift_of = jnp.arange(columns, dtype=jnp.int32) + me * columns
    place_of = L2 * jnp.arange(L1, dtype=jnp.int32)[:, None] + shift_of[None, :]
    valid_mask = place_of[None] < lengths[:, None, None]
    logits = out_rows.astype(F32)
    label_rows = labels.transpose(0, 2, 1)
    highest = jnp.max(logits, axis=-1)
    powers = jnp.exp(logits - highest[..., None])
    denominator = jnp.sum(powers, axis=-1)
    features = jnp.arange(D, dtype=jnp.int32)
    top = jnp.sum(jnp.where(features == label_rows[..., None], powers, 0.0), axis=-1)
    chance = top / denominator
    weight = (picked.astype(F32) * valid_mask.astype(F32)).transpose(0, 2, 1)
    sums = jnp.stack([jnp.sum(weight * chance), jnp.sum(weight)])
    sums = jnp.pad(sums, (0, D - 2))[None]
    rest = jnp.concatenate(
        [
            jnp.stack(
                [grad_bias_two, grad_shift_one, grad_shift_two, grad_gain_one, grad_gain_two]
            ),
            ordered,
            sums,
        ]
    )
    rest = lax.psum(rest, ("batch", "seq"))
    slice_of = D // (lax.axis_size("batch") * groups)
    norms = lax.dynamic_slice_in_dim(rest[:5], here * slice_of, slice_of, axis=1)
    grad_b_in = lax.dynamic_slice_in_dim(rest[5:-1].reshape(-1), here * share, share, axis=0)
    match_rate = D * rest[-1, 0] / jnp.maximum(rest[-1, 1], 1.0)
    return (
        current,
        input_grad,
        grad_first.T[None],
        grad_b_in[None],
        grad_second[None],
        norms[:3][None],
        norms[3:][None],
        match_rate,
    )


def solution(mesh):
    in_specs = (
        P("batch", None, "seq", None),
        P("batch"),
        P("batch", None, "seq"),
        P("batch", None, "seq"),
        P("batch", None, "seq", None),
        P(None, None, ("batch", "seq")),
        P(None, ("batch", "seq")),
        P(None, ("batch", "seq"), None),
        P(None, None, ("batch", "seq")),
        P(None, None, ("batch", "seq")),
    )
    out_specs = (
        P("batch", None, "seq", None),
        P("batch", None, "seq", None),
        P(None, None, ("batch", "seq")),
        P(None, ("batch", "seq")),
        P(None, ("batch", "seq"), None),
        P(None, None, ("batch", "seq")),
        P(None, None, ("batch", "seq")),
        P(),
    )
    return jax.shard_map(body, mesh=mesh, in_specs=in_specs, out_specs=out_specs, check_vma=False)
```

profile of v0, /device:TPU:0, one launch (start us, length us, event | category | flops | bytes accessed | tf_op | source)
XLA Modules:
  0.0 656.5 jit_solution(15531649239720909190)
XLA Ops:
  5.8 13.3 %collective-permute-done = bf16[1,2,96,768]{3,2,1,0:T(8,128)(2,1)S(1)} collective-permute-done((bf16[1,2,96,768]{3,2,1,0:T(8,128)(2,1)S(1)}, bf16[1,2,96,768]{3,2,1,0:T(8,128)(2,1)S(1)}, u32[]{:S(2)}, u32[]{:S(2)}) %collective-permute-start) | collective-permute-done | bytes 294944 | tf_op jit(solution)/shard_map/ppermute | solution.py:49
  20.0 13.8 %collective-permute-done.1 = bf16[2,2,96,768]{3,2,1,0:T(8,128)(2,1)S(1)} collective-permute-done((bf16[2,2,96,768]{3,2,1,0:T(8,128)(2,1)S(1)}, bf16[2,2,96,768]{3,2,1,0:T(8,128)(2,1)S(1)}, u32[]{:S(2)}, u32[]{:S(2)}) %collective-permute-start.1) | collective-permute-done | bytes 589856 | tf_op jit(solution)/shard_map/ppermute | solution.py:49
  33.9 6.6 %all-to-all-start = ((bf16[16,64,2,768]{3,2,1,0:T(2,128)(2,1)}), bf16[16,64,2,768]{3,2,1,0:T(2,128)(2,1)}, u32[]{:S(2)}, u32[]{:S(2)}) async-start(bf16[16,64,2,768]{3,2,1,0:T(2,128)(2,1)} %param.11), calls=%async_computation | async-start | bytes 6291456 | tf_op jit(solution)/shard_map/all_to_all | solution.py:112
  47.2 55.5 %collective-permute-done.2 = bf16[4,2,96,768]{3,2,1,0:T(8,128)(2,1)S(1)} collective-permute-done((bf16[4,2,96,768]{3,2,1,0:T(8,128)(2,1)S(1)}, bf16[4,2,96,768]{3,2,1,0:T(8,128)(2,1)S(1)}, u32[]{:S(2)}, u32[]{:S(2)}) %collective-permute-start.2) | collective-permute-done | bytes 1179680 | tf_op jit(solution)/shard_map/ppermute | solution.py:49
  106.1 83.7 %all-reduce.1 = bf16[3840]{0:T(1024)(128)(2,1)S(1)} all-reduce(bf16[3840]{0:T(1024)(128)(2,1)S(1)} %dynamic-update-slice), channel_id=2, replica_groups=mesh['batch'=2,'seq'=16] {'batch','seq'}, use_global_device_ids=true, to_apply=%add.1 | all-reduce | flops 3840 | bytes 15360
  190.8 10.0 %fusion.34 = bf16[1,768,768]{2,1,0:T(8,128)(2,1)} fusion(), kind=kLoop, calls=%fused_computation.87 | loop fusion | flops 8257536 | bytes 1179648 | tf_op jit(solution)/shard_map/neg | solution.py:110
  200.9 9.9 %multiply_convert_fusion.2 = bf16[1,768,768]{2,1,0:T(8,128)(2,1)} fusion(), kind=kLoop, calls=%fused_computation.82 | loop fusion | flops 6488064 | bytes 1179648 | tf_op jit(solution)/shard_map/convert_element_type | solution.py:36
  235.1 5.8 all-to-all-start.2
  252.7 7.2 %fusion.73 = (f32[32,64]{1,0:T(8,128)S(1)}, f32[32,64,768]{2,1,0:T(8,128)}) fusion(bf16[32,2,64,768]{3,2,1,0:T(8,128)(2,1)S(1)} %bitcast.161, bf16[1,768,768]{2,1,0:T(8,128)(2,1)S(1)} %copy-done.10, bf16[1,768,768]{2,1,0:T(8,128)(2,1)S(1)} %copy-done.12, bf16[32,64,768]{2,1,0:T(8,128)(2,1)S(1)} %bitcast_select_fusion), kind=kOutput, calls=%fused_computation.198 | convolution fusion | flops 4837734400 | bytes 18096128 | tf_op jit(solution)/shard_map/lund,ude->lne/dot_general | solution.py:127
  268.4 5.0 constant_dynamic-update-slice_fusion
  273.4 8.0 %fusion.70 = (bf16[32,1,96,768]{3,2,1,0:T(8,128)(2,1)}, bf16[32,1,96,768]{3,2,1,0:T(8,128)(2,1)}) fusion(bf16[32,2,96,768]{3,2,1,0:T(8,128)(2,1)} %constant_dynamic-update-slice_fusion), kind=kLoop, calls=%fused_computation.195 | loop fusion | bytes 18874368 | tf_op jit(solution)/shard_map/slice | solution.py:96
  281.4 24.9 %multiply_convert_fusion = (bf16[2048,3072]{1,0:T(8,128)(2,1)}, f32[2048,3072]{1,0:T(8,128)}) fusion(f32[3072]{0:T(1024)S(1)} %add.303, bf16[2048,768]{1,0:T(8,128)(2,1)} %bitcast.169, bf16[3072,768]{1,0:T(8,128)(2,1)} %bitcast.162), kind=kOutput, calls=%fused_computation.9 | convolution fusion | flops 9726590976 | bytes 45625344 | tf_op jit(solution)/shard_map/td,fd->tf/dot_general | solution.py:131
  306.3 16.2 %fusion.74 = (f32[2048]{0:T(1024)S(1)}, f32[2048,768]{1,0:T(8,128)S(1)}) fusion(f32[768]{0:T(1024)S(1)} %add.309, bf16[2048,3072]{1,0:T(8,128)(2,1)} %get-tuple-element.82, bf16[3072,768]{1,0:T(8,128)(2,1)} %bitcast.164, f32[768]{0:T(1024)S(1)} %add.298, f32[768]{0:T(1024)S(1)} %mul.622, f32[2048]{0:T(1024)S(1)} %rsqrt.25, f32[2048]{0:T(1024)S(1)} %div.52, ...), kind=kOutput, calls=%fused_computation.199 | convolution fusion | flops 9674684416 | bytes 29918208 | tf_op jit(solution)/shard_map/dot_general | solution.py:133
  338.3 17.8 %fusion.67 = f32[3072,768]{1,0:T(8,128)} fusion(bf16[2048,3072]{1,0:T(8,128)(2,1)} %get-tuple-element.82, f32[2048,768]{1,0:T(8,128)S(1)} %get-tuple-element.63, f32[2048]{0:T(1024)S(1)} %negate_multiply_fusion.1), kind=kOutput, calls=%fused_computation.192 | convolution fusion | flops 9666822144 | bytes 28319744 | tf_op jit(solution)/shard_map/tf,td->fd/dot_general | solution.py:143
  356.1 34.4 %fusion.75 = (f32[3072]{0:T(1024)S(1)}, bf16[2048,3072]{1,0:T(8,128)(2,1)}) fusion(bf16[3072,768]{1,0:T(8,128)(2,1)} %bitcast.165, f32[2048,768]{1,0:T(8,128)S(1)} %get-tuple-element.63, f32[2048]{0:T(1024)S(1)} %negate_multiply_fusion.1, f32[2048,3072]{1,0:T(8,128)} %get-tuple-element.83, f32[3072]{0:T(1024)S(1)} %add.303), kind=kOutput, calls=%fused_computation.200 | convolution fusion | flops 9830396928 | bytes 48791552 | tf_op jit(solution)/shard_map/td,fd->tf/dot_general | solution.py:144
  390.5 6.8 %copy.55 = bf16[16,2,64,768]{3,1,2,0:T(2,128)(2,1)} copy(bf16[16,2,64,768]{3,2,1,0:T(8,128)(2,1)} %bitcast.156) | data formatting | bytes 6291456 | tf_op jit(solution)/shard_map/reshape | solution.py:135
  397.4 17.3 %multiply_reduce_fusion = (f32[768]{0:T(1024)S(1)}, f32[2048]{0:T(1024)S(1)}, f32[768]{0:T(1024)S(1)}, f32[2048,768]{1,0:T(8,128)}) fusion(f32[32,64,768]{2,1,0:T(8,128)S(1)} %bitcast.144, f32[2048]{0:T(1024)S(1)} %rsqrt.25, f32[2048]{0:T(1024)S(1)} %div.52, f32[768]{0:T(1024)S(1)} %mul.622, bf16[3072,768]{1,0:T(8,128)(2,1)} %bitcast.163, ...), kind=kOutput, calls=%fused_computation.39 | convolution fusion | flops 9679400960 | bytes 36217856 | tf_op jit(solution)/shard_map/dot_general | solution.py:150
  414.7 6.5 all-to-all-start.1
  421.2 7.2 %fusion.68 = (f32[2048]{0:T(1024)S(1)}, f32[2048,768]{1,0:T(8,128)S(1)}, bf16[2048,768]{1,0:T(8,128)(2,1)}) fusion(f32[2048]{0:T(1024)S(1)} %multiply_multiply_fusion.2, f32[2048]{0:T(1024)S(1)} %div.52, f32[32,64,768]{2,1,0:T(8,128)} %get-tuple-element.81, f32[2048]{0:T(1024)S(1)} %rsqrt.25, f32[2048,768]{1,0:T(8,128)} %get-tuple-element.86, ...), kind=kLoop, calls=%fused_computation.193 | loop fusion | flops 17299456 | bytes 22059008 | tf_op jit(solution)/shard_map/transpose(jvp())/reduce_sum | solution.py:18
  428.5 14.2 %fusion.17 = f32[3072,768]{1,0:T(8,128)S(1)} fusion(bf16[2048,768]{1,0:T(8,128)(2,1)} %get-tuple-element.70, bf16[2048,3072]{1,0:T(8,128)(2,1)} %get-tuple-element.88), kind=kOutput, calls=%fused_computation.43 | convolution fusion | flops 9663676416 | bytes 25165824 | tf_op jit(solution)/shard_map/tf,td->fd/dot_general | solution.py:149
  448.9 8.9 %convert_bitcast_fusion.1 = bf16[32,2,64,768]{3,2,0,1:T(8,128)(2,1)} fusion(bf16[32,64,768,1]{2,1,0,3:T(8,128)(2,1)} %bitcast.167, bf16[1,768,768]{2,1,0:T(8,128)(2,1)S(1)} %copy-done.11, bf16[1,768,768]{2,1,0:T(8,128)(2,1)} %multiply_convert_fusion.2), kind=kOutput, calls=%fused_computation.40 | convolution fusion | flops 4839702528 | bytes 11796480 | tf_op jit(solution)/shard_map/lne,ude->lund/dot_general | solution.py:154
  481.5 4.9 copy.60
  486.4 9.9 %all-to-all-start.3 = ((bf16[16,2,64,768]{3,1,2,0:T(2,128)(2,1)}), bf16[16,2,64,768]{3,1,2,0:T(2,128)(2,1)}, u32[]{:S(2)}, u32[]{:S(2)}) async-start(bf16[16,2,64,768]{3,1,2,0:T(2,128)(2,1)} %copy.60), calls=%async_computation.3 | async-start | bytes 6291456 | tf_op jit(solution)/shard_map/all_to_all | solution.py:168
  508.4 19.2 %collective-permute-done.11 = bf16[8,96,768]{2,1,0:T(8,128)(2,1)} collective-permute-done((bf16[8,96,768]{2,1,0:T(8,128)(2,1)}, bf16[8,96,768]{2,1,0:T(8,128)(2,1)}, u32[]{:S(2)}, u32[]{:S(2)}) %collective-permute-start.11) | collective-permute-done | bytes 1179680 | tf_op jit(solution)/shard_map/ppermute | solution.py:49
  532.2 5.6 collective-permute-done.17
  538.7 19.7 %collective-permute-done.12 = bf16[4,96,768]{2,1,0:T(8,128)(2,1)S(1)} collective-permute-done((bf16[4,96,768]{2,1,0:T(8,128)(2,1)S(1)}, bf16[4,96,768]{2,1,0:T(8,128)(2,1)S(1)}, u32[]{:S(2)}, u32[]{:S(2)}) %collective-permute-start.12) | collective-permute-done | bytes 589856 | tf_op jit(solution)/shard_map/ppermute | solution.py:49
  561.3 7.2 %collective-permute-done.13 = bf16[2,96,768]{2,1,0:T(8,128)(2,1)} collective-permute-done((bf16[2,96,768]{2,1,0:T(8,128)(2,1)}, bf16[2,96,768]{2,1,0:T(8,128)(2,1)}, u32[]{:S(2)}, u32[]{:S(2)}) %collective-permute-start.13) | collective-permute-done | bytes 294944 | tf_op jit(solution)/shard_map/ppermute | solution.py:49
  569.7 8.5 %collective-permute-start.14 = (bf16[1,96,768]{2,1,0:T(8,128)(2,1)S(1)}, bf16[1,96,768]{2,1,0:T(8,128)(2,1)S(1)}, u32[]{:S(2)}, u32[]{:S(2)}) collective-permute-start(bf16[1,96,768]{2,1,0:T(8,128)(2,1)S(1)} %slice.266), channel_id=1, source_target_pairs={{0,8},{1,9},{2,10},{3,11},{4,12},{5,13},{6,14},{7,15},{8,0},{9,1},... | collective-permute-start | bytes 442376 | tf_op jit(solution)/shard_map/ppermute | solution.py:49
  579.0 6.4 collective-permute-done.14
  588.7 13.2 %fusion.22 = (f32[16,2,64]{1,2,0:T(8,128)S(1)}, f32[16,2,64]{1,2,0:T(8,128)S(1)}) fusion(bf16[16,2,64,768]{3,1,2,0:T(2,128)(2,1)S(1)} %all-to-all-done.1, f32[16,2,64]{1,2,0:T(8,128)S(1)} %reduce_max.15, s32[16,2,64]{1,2,0:T(8,128)} %copy.62), kind=kLoop, calls=%fused_computation.60 | loop fusion | flops 9433088 | bytes 3178496 | tf_op jit(solution)/shard_map/reduce_sum | solution.py:195
  604.3 39.5 %psum.7 = f32[10,768]{1,0:T(8,128)S(1)} all-reduce(f32[10,768]{1,0:T(8,128)S(1)} %concatenate.64), channel_id=1, replica_groups=mesh['batch'=2,'seq'=16] {'batch','seq'}, use_global_device_ids=true, to_apply=%region_20.21 | all-reduce | flops 7680 | bytes 61440 | tf_op jit(solution)/shard_map/psum | solution.py:211
  649.3 5.9 copy.77
  (264 shorter events, 139.1 us)
Async XLA Ops:
  0.6 45.3 %copy-start.36 = (s32[32]{0:T(128)S(1)}, s32[32]{0:T(128)}, u32[]{:S(2)}) copy-start(s32[32]{0:T(128)} %constant.129.clone) | copy-start | bytes 388
  0.7 42.8 %copy-start.34 = (bf16[1,3,24]{2,1,0:T(4,128)(2,1)S(1)}, bf16[1,3,24]{2,1,0:T(4,128)(2,1)}, u32[]{:S(2)}) copy-start(bf16[1,3,24]{2,1,0:T(4,128)(2,1)} %param.19) | copy-start | bytes 436
  0.7 42.9 %copy-start.35 = (bf16[1,2,24]{2,1,0:T(2,128)(2,1)S(1)}, bf16[1,2,24]{2,1,0:T(2,128)(2,1)}, u32[]{:S(2)}) copy-start(bf16[1,2,24]{2,1,0:T(2,128)(2,1)} %param.20) | copy-start | bytes 292
  0.7 42.9 %copy-start.32 = (s32[16]{0:T(128)S(1)}, s32[16]{0:T(128)}, u32[]{:S(2)}) copy-start(s32[16]{0:T(128)} %param.12) | copy-start | bytes 196
  1.7 17.4 %collective-permute-start = (bf16[1,2,96,768]{3,2,1,0:T(8,128)(2,1)S(1)}, bf16[1,2,96,768]{3,2,1,0:T(8,128)(2,1)S(1)}, u32[]{:S(2)}, u32[]{:S(2)}) collective-permute-start(bf16[1,2,96,768]{3,2,1,0:T(8,128)(2,1)S(1)} %maximum_bitcast_fusion.1), channel_id=1, source_target_pairs={{0,8},{1,9},{2,10},{3,11},{4,12},{5,13},{6,14},{7,15},{8,0},{9,1},... | collective-permute-start | bytes 884744 | tf_op jit(solution)/shard_map/ppermute | solution.py:49
  19.2 14.6 %collective-permute-start.1 = (bf16[2,2,96,768]{3,2,1,0:T(8,128)(2,1)S(1)}, bf16[2,2,96,768]{3,2,1,0:T(8,128)(2,1)S(1)}, u32[]{:S(2)}, u32[]{:S(2)}) collective-permute-start(bf16[2,2,96,768]{3,2,1,0:T(8,128)(2,1)S(1)} %pad_maximum_fusion.6), channel_id=1, source_target_pairs={{0,4},{1,5},{2,6},{3,7},{4,0},{5,1},{6,2},{7,3},{8,12},{9,13},{10,... | collective-permute-start | bytes 1769480 | tf_op jit(solution)/shard_map/ppermute | solution.py:49
  33.9 185.7 %copy-start.28 = (s32[16,64,2]{1,2,0:T(2,128)S(1)}, s32[16,64,2]{1,2,0:T(2,128)}, u32[]{:S(2)}) copy-start(s32[16,64,2]{1,2,0:T(2,128)} %param.14) | copy-start | bytes 24580
  33.9 197.0 %all-to-all-start = ((bf16[16,64,2,768]{3,2,1,0:T(2,128)(2,1)}), bf16[16,64,2,768]{3,2,1,0:T(2,128)(2,1)}, u32[]{:S(2)}, u32[]{:S(2)}) async-start(bf16[16,64,2,768]{3,2,1,0:T(2,128)(2,1)} %param.11), calls=%async_computation | async-start | bytes 6291456 | tf_op jit(solution)/shard_map/all_to_all | solution.py:112
  40.6 160.3 %collective-permute-start.5 = (f32[1,96]{1,0:T(1,128)S(1)}, f32[1,96]{1,0:T(1,128)S(1)}, u32[]{:S(2)}, u32[]{:S(2)}) collective-permute-start(f32[1,96]{1,0:T(1,128)S(1)} %convert_element_type.301), channel_id=1, source_target_pairs={{0,8},{1,9},{2,10},{3,11},{4,12},{5,13},{6,14},{7,15},{8,0},{9,1},... | collective-permute-start | bytes 1160 | tf_op jit(solution)/shard_map/ppermute | solution.py:49
  44.2 58.4 %collective-permute-start.2 = (bf16[4,2,96,768]{3,2,1,0:T(8,128)(2,1)S(1)}, bf16[4,2,96,768]{3,2,1,0:T(8,128)(2,1)S(1)}, u32[]{:S(2)}, u32[]{:S(2)}) collective-permute-start(bf16[4,2,96,768]{3,2,1,0:T(8,128)(2,1)S(1)} %pad_maximum_fusion.5), channel_id=1, source_target_pairs={{0,2},{1,3},{2,0},{3,1},{4,6},{5,7},{6,4},{7,5},{8,10},{9,11},{10,... | collective-permute-start | bytes 3538952 | tf_op jit(solution)/shard_map/ppermute | solution.py:49
  46.6 194.4 %copy-start.29 = (pred[32,64]{1,0:T(8,128)(4,1)}, pred[32,64]{1,0:T(8,128)(4,1)S(1)}, u32[]{:S(2)}) copy-start(pred[32,64]{1,0:T(8,128)(4,1)S(1)} %add_compare_fusion) | copy-start | bytes 6148
  104.3 119.2 %collective-permute-start.3 = (bf16[8,2,96,768]{3,2,1,0:T(8,128)(2,1)}, bf16[8,2,96,768]{3,2,1,0:T(8,128)(2,1)}, u32[]{:S(2)}, u32[]{:S(2)}) collective-permute-start(bf16[8,2,96,768]{3,2,1,0:T(8,128)(2,1)} %pad_maximum_fusion.2), channel_id=1, source_target_pairs={{0,16},{16,0},{1,17},{17,1},{2,18},{18,2},{3,19},{19,3},{4,20},{20... | collective-permute-start | bytes 7077896 | tf_op jit(solution)/shard_map/ppermute | solution.py:49
  200.9 10.0 %collective-permute-start.6 = (f32[2,96]{1,0:T(2,128)S(1)}, f32[2,96]{1,0:T(2,128)S(1)}, u32[]{:S(2)}, u32[]{:S(2)}) collective-permute-start(f32[2,96]{1,0:T(2,128)S(1)} %pad_maximum_fusion.10), channel_id=1, source_target_pairs={{0,4},{1,5},{2,6},{3,7},{4,0},{5,1},{6,2},{7,3},{8,12},{9,13},{10,... | collective-permute-start | bytes 2312 | tf_op jit(solution)/shard_map/ppermute | solution.py:49
  210.9 3.9 collective-permute-start.7
  214.8 3.7 collective-permute-start.8
  218.5 2.7 collective-permute-start.9
  227.2 41.2 %collective-permute-start.4 = (bf16[16,2,96,768]{3,2,1,0:T(8,128)(2,1)}, bf16[16,2,96,768]{3,2,1,0:T(8,128)(2,1)}, u32[]{:S(2)}, u32[]{:S(2)}) collective-permute-start(bf16[16,2,96,768]{3,2,1,0:T(8,128)(2,1)} %pad_maximum_fusion), channel_id=1, source_target_pairs={{0,1},{1,0},{2,3},{3,2},{4,5},{5,4},{6,7},{7,6},{8,9},{9,8},{10,11... | collective-permute-start | bytes 14155784 | tf_op jit(solution)/shard_map/ppermute | solution.py:49
  235.1 90.8 %all-to-all-start.2 = ((bf16[16,64,2,768]{3,2,1,0:T(2,128)(2,1)}), bf16[16,64,2,768]{3,2,1,0:T(2,128)(2,1)S(1)}, u32[]{:S(2)}, u32[]{:S(2)}) async-start(bf16[16,64,2,768]{3,2,1,0:T(2,128)(2,1)} %param.15), calls=%async_computation.2 | async-start | bytes 6291456 | tf_op jit(solution)/shard_map/all_to_all | solution.py:114
  338.3 59.0 %copy-start.2 = (f32[2048,768]{1,0:T(8,128)}, f32[2048,768]{1,0:T(8,128)S(1)}, u32[]{:S(2)}) copy-start(f32[2048,768]{1,0:T(8,128)S(1)} %get-tuple-element.63) | copy-start | bytes 18874372
  356.1 41.2 %slice-start.3 = ((s8[6291456]{0:T(1024)(128)(4,1)}), s8[2097152]{0:T(1024)(128)(4,1)S(1)}, s32[]{:S(2)}) async-start(s8[6291456]{0:T(1024)(128)(4,1)} %bitcast.143), calls=%async_computation.7 | async-start | bytes 4194304
  414.7 71.7 %all-to-all-start.1 = ((bf16[16,2,64,768]{3,1,2,0:T(2,128)(2,1)}), bf16[16,2,64,768]{3,1,2,0:T(2,128)(2,1)S(1)}, u32[]{:S(2)}, u32[]{:S(2)}) async-start(bf16[16,2,64,768]{3,1,2,0:T(2,128)(2,1)} %copy.55), calls=%async_computation.1 | async-start | bytes 6291456 | tf_op jit(solution)/shard_map/all_to_all | solution.py:136
  446.1 23.4 %collective-permute-start.15 = (bf16[16,96,768]{2,1,0:T(8,128)(2,1)}, bf16[16,96,768]{2,1,0:T(8,128)(2,1)}, u32[]{:S(2)}, u32[]{:S(2)}) collective-permute-start(bf16[16,96,768]{2,1,0:T(8,128)(2,1)} %bitcast.57), channel_id=1, source_target_pairs={{0,1},{1,0},{2,3},{3,2},{4,5},{5,4},{6,7},{7,6},{8,9},{9,8},{10,11... | collective-permute-start | bytes 7077896 | tf_op jit(solution)/shard_map/ppermute | solution.py:49
  446.6 27.6 %collective-permute-start.10 = (bf16[16,96,768]{2,1,0:T(8,128)(2,1)}, bf16[16,96,768]{2,1,0:T(8,128)(2,1)}, u32[]{:S(2)}, u32[]{:S(2)}) collective-permute-start(bf16[16,96,768]{2,1,0:T(8,128)(2,1)} %bitcast.47), channel_id=1, source_target_pairs={{0,1},{1,0},{2,3},{3,2},{4,5},{5,4},{6,7},{7,6},{8,9},{9,8},{10,11... | collective-permute-start | bytes 7077896 | tf_op jit(solution)/shard_map/ppermute | solution.py:49
  473.7 30.2 %collective-permute-start.16 = (bf16[8,96,768]{2,1,0:T(8,128)(2,1)}, bf16[8,96,768]{2,1,0:T(8,128)(2,1)}, u32[]{:S(2)}, u32[]{:S(2)}) collective-permute-start(bf16[8,96,768]{2,1,0:T(8,128)(2,1)} %slice.259), channel_id=1, source_target_pairs={{0,16},{16,0},{1,17},{17,1},{2,18},{18,2},{3,19},{19,3},{4,20},{20... | collective-permute-start | bytes 3538952 | tf_op jit(solution)/shard_map/ppermute | solution.py:49
  478.1 49.5 %collective-permute-start.11 = (bf16[8,96,768]{2,1,0:T(8,128)(2,1)}, bf16[8,96,768]{2,1,0:T(8,128)(2,1)}, u32[]{:S(2)}, u32[]{:S(2)}) collective-permute-start(bf16[8,96,768]{2,1,0:T(8,128)(2,1)} %slice.260), channel_id=1, source_target_pairs={{0,16},{16,0},{1,17},{17,1},{2,18},{18,2},{3,19},{19,3},{4,20},{20... | collective-permute-start | bytes 3538952 | tf_op jit(solution)/shard_map/ppermute | solution.py:49
  486.4 159.3 %all-to-all-start.3 = ((bf16[16,2,64,768]{3,1,2,0:T(2,128)(2,1)}), bf16[16,2,64,768]{3,1,2,0:T(2,128)(2,1)}, u32[]{:S(2)}, u32[]{:S(2)}) async-start(bf16[16,2,64,768]{3,1,2,0:T(2,128)(2,1)} %copy.60), calls=%async_computation.3 | async-start | bytes 6291456 | tf_op jit(solution)/shard_map/all_to_all | solution.py:168
  506.3 31.4 %collective-permute-start.17 = (bf16[4,96,768]{2,1,0:T(8,128)(2,1)S(1)}, bf16[4,96,768]{2,1,0:T(8,128)(2,1)S(1)}, u32[]{:S(2)}, u32[]{:S(2)}) collective-permute-start(bf16[4,96,768]{2,1,0:T(8,128)(2,1)S(1)} %slice.261), channel_id=1, source_target_pairs={{0,2},{1,3},{2,0},{3,1},{4,6},{5,7},{6,4},{7,5},{8,10},{9,11},{10,... | collective-permute-start | bytes 1769480 | tf_op jit(solution)/shard_map/ppermute | solution.py:49
  530.0 28.4 %collective-permute-start.12 = (bf16[4,96,768]{2,1,0:T(8,128)(2,1)S(1)}, bf16[4,96,768]{2,1,0:T(8,128)(2,1)S(1)}, u32[]{:S(2)}, u32[]{:S(2)}) collective-permute-start(bf16[4,96,768]{2,1,0:T(8,128)(2,1)S(1)} %slice.262), channel_id=1, source_target_pairs={{0,2},{1,3},{2,0},{3,1},{4,6},{5,7},{6,4},{7,5},{8,10},{9,11},{10,... | collective-permute-start | bytes 1769480 | tf_op jit(solution)/shard_map/ppermute | solution.py:49
  538.7 21.3 %collective-permute-start.18 = (bf16[2,96,768]{2,1,0:T(8,128)(2,1)}, bf16[2,96,768]{2,1,0:T(8,128)(2,1)}, u32[]{:S(2)}, u32[]{:S(2)}) collective-permute-start(bf16[2,96,768]{2,1,0:T(8,128)(2,1)} %slice.263), channel_id=1, source_target_pairs={{0,4},{1,5},{2,6},{3,7},{4,0},{5,1},{6,2},{7,3},{8,12},{9,13},{10,... | collective-permute-start | bytes 884744 | tf_op jit(solution)/shard_map/ppermute | solution.py:49
  559.6 8.9 %collective-permute-start.13 = (bf16[2,96,768]{2,1,0:T(8,128)(2,1)}, bf16[2,96,768]{2,1,0:T(8,128)(2,1)}, u32[]{:S(2)}, u32[]{:S(2)}) collective-permute-start(bf16[2,96,768]{2,1,0:T(8,128)(2,1)} %slice.264), channel_id=1, source_target_pairs={{0,4},{1,5},{2,6},{3,7},{4,0},{5,1},{6,2},{7,3},{8,12},{9,13},{10,... | collective-permute-start | bytes 884744 | tf_op jit(solution)/shard_map/ppermute | solution.py:49
  561.2 17.0 %collective-permute-start.19 = (bf16[1,96,768]{2,1,0:T(8,128)(2,1)S(1)}, bf16[1,96,768]{2,1,0:T(8,128)(2,1)S(1)}, u32[]{:S(2)}, u32[]{:S(2)}) collective-permute-start(bf16[1,96,768]{2,1,0:T(8,128)(2,1)S(1)} %slice.265), channel_id=1, source_target_pairs={{0,8},{1,9},{2,10},{3,11},{4,12},{5,13},{6,14},{7,15},{8,0},{9,1},... | collective-permute-start | bytes 442376 | tf_op jit(solution)/shard_map/ppermute | solution.py:49
  569.7 15.6 %collective-permute-start.14 = (bf16[1,96,768]{2,1,0:T(8,128)(2,1)S(1)}, bf16[1,96,768]{2,1,0:T(8,128)(2,1)S(1)}, u32[]{:S(2)}, u32[]{:S(2)}) collective-permute-start(bf16[1,96,768]{2,1,0:T(8,128)(2,1)S(1)} %slice.266), channel_id=1, source_target_pairs={{0,8},{1,9},{2,10},{3,11},{4,12},{5,13},{6,14},{7,15},{8,0},{9,1},... | collective-permute-start | bytes 442376 | tf_op jit(solution)/shard_map/ppermute | solution.py:49
  (40 other events, 546.8 us)
where the time goes:
time: 663 us; the launch traced here: 657 us
  matrix products  148 us (22%)
  waiting for transfers between devices  143 us (22%)
  blocking collectives  123 us (19%)
  other arithmetic  103 us (16%)
  local copies, waits for them, and re-layouts  74.2 us (11%)
  starting transfers between devices  59.6 us (9%)
    ppermute x20, waiting for transfers between devices, swap(): return lax.ppermute(values, axis, [(i, i ^ mask) for i in range(size)])  143 us
    unnamed x1, blocking collectives  83.7 us
    psum x1, blocking collectives, body(): rest = lax.psum(rest, ('batch', 'seq'))  39.5 us
    dot_general x1, matrix products, body(): jnp.einsum('td,fd->tf', summed_low, w_second, preferred_element_type=F32)  34.4 us
    ppermute x20, starting transfers between devices, swap(): return lax.ppermute(values, axis, [(i, i ^ mask) for i in range(size)])  30.7 us
    dot_general x1, matrix products, body(): jnp.einsum('td,fd->tf', normed_low, w_first, preferred_element_type=F32)  24.9 us
    unnamed x100, local copies, waits for them, and re-layouts  18.2 us
    dot_general x1, matrix products, body(): jnp.einsum('tf,td->fd', act_low, summed_low, preferred_element_type=F32)  17.8 us
  transfers between devices with their start and end apart: 24, of which 10 were waited for; matrix products, arithmetic and copies ran while one was open for 34% of the time, Pallas kernels for 0%

commit v1 on v0

--- a/solution.py
+++ b/solution.py
@@ -208,7 +208,7 @@
             sums,
         ]
     )
-    rest = lax.psum(rest, ("batch", "seq"))
+    rest = lax.psum(lax.psum(rest, "seq"), "batch")
     slice_of = D // (lax.axis_size("batch") * groups)
     norms = lax.dynamic_slice_in_dim(rest[:5], here * slice_of, slice_of, axis=1)
     grad_b_in = lax.dynamic_slice_in_dim(rest[5:-1].reshape(-1), here * share, share, axis=0)

time: 663 us -> 689 us (1.039)
  blocking collectives: 123 us -> 149 us
    psum x1 -> x2, blocking collectives: 39.5 us -> 65.6 us  [body(): rest = lax.psum(lax.psum(rest, 'seq'), 'batch')]
  transfers between devices with their start and end apart: 24 -> 24, of which waited for: 10 -> 10; matrix products, arithmetic and copies ran while one was open for 34% -> 33% of each run, Pallas kernels for 0% -> 0%
where the time goes in v1:
time: 689 us; the launch traced here: 683 us
  blocking collectives  149 us (22%)
  matrix products  148 us (21%)
  waiting for transfers between devices  143 us (21%)
  other arithmetic  103 us (15%)
  local copies, waits for them, and re-layouts  74.2 us (11%)
  starting transfers between devices  59.5 us (9%)
    ppermute x20, waiting for transfers between devices, swap(): return lax.ppermute(values, axis, [(i, i ^ mask) for i in range(size)])  143 us
    unnamed x1, blocking collectives  83.7 us
    psum x2, blocking collectives, body(): rest = lax.psum(lax.psum(rest, 'seq'), 'batch')  65.6 us
    dot_general x1, matrix products, body(): jnp.einsum('td,fd->tf', summed_low, w_second, preferred_element_type=F32)  34.4 us
    ppermute x20, starting transfers between devices, swap(): return lax.ppermute(values, axis, [(i, i ^ mask) for i in range(size)])  30.7 us
    dot_general x1, matrix products, body(): jnp.einsum('td,fd->tf', normed_low, w_first, preferred_element_type=F32)  24.9 us
    unnamed x100, local copies, waits for them, and re-layouts  18.2 us
    dot_general x1, matrix products, body(): jnp.einsum('tf,td->fd', act_low, summed_low, preferred_element_type=F32)  17.8 us
  transfers between devices with their start and end apart: 24, of which 10 were waited for; matrix products, arithmetic and copies ran while one was open for 33% of the time, Pallas kernels for 0%

profile of v1, /device:TPU:0, one launch (start us, length us, event | category | flops | bytes accessed | tf_op | source)
XLA Modules:
  0.0 682.6 jit_solution(4382830192867453282)
XLA Ops:
  5.8 13.3 %collective-permute-done = bf16[1,2,96,768]{3,2,1,0:T(8,128)(2,1)S(1)} collective-permute-done((bf16[1,2,96,768]{3,2,1,0:T(8,128)(2,1)S(1)}, bf16[1,2,96,768]{3,2,1,0:T(8,128)(2,1)S(1)}, u32[]{:S(2)}, u32[]{:S(2)}) %collective-permute-start) | collective-permute-done | bytes 294944 | tf_op jit(solution)/shard_map/ppermute | solution.py:49
  20.0 13.8 %collective-permute-done.1 = bf16[2,2,96,768]{3,2,1,0:T(8,128)(2,1)S(1)} collective-permute-done((bf16[2,2,96,768]{3,2,1,0:T(8,128)(2,1)S(1)}, bf16[2,2,96,768]{3,2,1,0:T(8,128)(2,1)S(1)}, u32[]{:S(2)}, u32[]{:S(2)}) %collective-permute-start.1) | collective-permute-done | bytes 589856 | tf_op jit(solution)/shard_map/ppermute | solution.py:49
  33.9 6.6 all-to-all-start
  47.2 55.5 %collective-permute-done.2 = bf16[4,2,96,768]{3,2,1,0:T(8,128)(2,1)S(1)} collective-permute-done((bf16[4,2,96,768]{3,2,1,0:T(8,128)(2,1)S(1)}, bf16[4,2,96,768]{3,2,1,0:T(8,128)(2,1)S(1)}, u32[]{:S(2)}, u32[]{:S(2)}) %collective-permute-start.2) | collective-permute-done | bytes 1179680 | tf_op jit(solution)/shard_map/ppermute | solution.py:49
  106.1 83.7 %all-reduce.1 = bf16[3840]{0:T(1024)(128)(2,1)S(1)} all-reduce(bf16[3840]{0:T(1024)(128)(2,1)S(1)} %dynamic-update-slice), channel_id=2, replica_groups=mesh['batch'=2,'seq'=16] {'batch','seq'}, use_global_device_ids=true, to_apply=%add.1 | all-reduce | flops 3840 | bytes 15360
  190.8 10.0 %fusion.34 = bf16[1,768,768]{2,1,0:T(8,128)(2,1)} fusion(), kind=kLoop, calls=%fused_computation.87 | loop fusion | flops 8257536 | bytes 1179648 | tf_op jit(solution)/shard_map/neg | solution.py:110
  200.9 9.9 %multiply_convert_fusion.2 = bf16[1,768,768]{2,1,0:T(8,128)(2,1)} fusion(), kind=kLoop, calls=%fused_computation.82 | loop fusion | flops 6488064 | bytes 1179648 | tf_op jit(solution)/shard_map/convert_element_type | solution.py:36
  235.1 5.8 all-to-all-start.2
  252.6 7.2 %fusion.73 = (f32[32,64]{1,0:T(8,128)S(1)}, f32[32,64,768]{2,1,0:T(8,128)}) fusion(bf16[32,2,64,768]{3,2,1,0:T(8,128)(2,1)S(1)} %bitcast.161, bf16[1,768,768]{2,1,0:T(8,128)(2,1)S(1)} %copy-done.10, bf16[1,768,768]{2,1,0:T(8,128)(2,1)S(1)} %copy-done.12, bf16[32,64,768]{2,1,0:T(8,128)(2,1)S(1)} %bitcast_select_fusion), kind=kOutput, calls=%fused_computation.198 | convolution fusion | flops 4837734400 | bytes 18096128 | tf_op jit(solution)/shard_map/lund,ude->lne/dot_general | solution.py:127
  268.4 4.9 constant_dynamic-update-slice_fusion
  273.3 8.0 %fusion.70 = (bf16[32,1,96,768]{3,2,1,0:T(8,128)(2,1)}, bf16[32,1,96,768]{3,2,1,0:T(8,128)(2,1)}) fusion(bf16[32,2,96,768]{3,2,1,0:T(8,128)(2,1)} %constant_dynamic-update-slice_fusion), kind=kLoop, calls=%fused_computation.195 | loop fusion | bytes 18874368 | tf_op jit(solution)/shard_map/slice | solution.py:96
  281.3 24.9 %multiply_convert_fusion = (bf16[2048,3072]{1,0:T(8,128)(2,1)}, f32[2048,3072]{1,0:T(8,128)}) fusion(f32[3072]{0:T(1024)S(1)} %add.305, bf16[2048,768]{1,0:T(8,128)(2,1)} %bitcast.169, bf16[3072,768]{1,0:T(8,128)(2,1)} %bitcast.162), kind=kOutput, calls=%fused_computation.9 | convolution fusion | flops 9726590976 | bytes 45625344 | tf_op jit(solution)/shard_map/td,fd->tf/dot_general | solution.py:131
  306.2 16.2 %fusion.74 = (f32[2048]{0:T(1024)S(1)}, f32[2048,768]{1,0:T(8,128)S(1)}) fusion(f32[768]{0:T(1024)S(1)} %add.311, bf16[2048,3072]{1,0:T(8,128)(2,1)} %get-tuple-element.82, bf16[3072,768]{1,0:T(8,128)(2,1)} %bitcast.164, f32[768]{0:T(1024)S(1)} %add.300, f32[768]{0:T(1024)S(1)} %mul.622, f32[2048]{0:T(1024)S(1)} %rsqrt.25, f32[2048]{0:T(1024)S(1)} %div.52, ...), kind=kOutput, calls=%fused_computation.199 | convolution fusion | flops 9674684416 | bytes 29918208 | tf_op jit(solution)/shard_map/dot_general | solution.py:133
  338.3 17.8 %fusion.67 = f32[3072,768]{1,0:T(8,128)} fusion(bf16[2048,3072]{1,0:T(8,128)(2,1)} %get-tuple-element.82, f32[2048,768]{1,0:T(8,128)S(1)} %get-tuple-element.63, f32[2048]{0:T(1024)S(1)} %negate_multiply_fusion.1), kind=kOutput, calls=%fused_computation.192 | convolution fusion | flops 9666822144 | bytes 28319744 | tf_op jit(solution)/shard_map/tf,td->fd/dot_general | solution.py:143
  356.1 34.4 %fusion.75 = (f32[3072]{0:T(1024)S(1)}, bf16[2048,3072]{1,0:T(8,128)(2,1)}) fusion(bf16[3072,768]{1,0:T(8,128)(2,1)} %bitcast.165, f32[2048,768]{1,0:T(8,128)S(1)} %get-tuple-element.63, f32[2048]{0:T(1024)S(1)} %negate_multiply_fusion.1, f32[2048,3072]{1,0:T(8,128)} %get-tuple-element.83, f32[3072]{0:T(1024)S(1)} %add.305), kind=kOutput, calls=%fused_computation.200 | convolution fusion | flops 9830396928 | bytes 48791552 | tf_op jit(solution)/shard_map/td,fd->tf/dot_general | solution.py:144
  390.5 6.8 copy.55
  397.3 17.3 %multiply_reduce_fusion = (f32[768]{0:T(1024)S(1)}, f32[2048]{0:T(1024)S(1)}, f32[768]{0:T(1024)S(1)}, f32[2048,768]{1,0:T(8,128)}) fusion(f32[32,64,768]{2,1,0:T(8,128)S(1)} %bitcast.144, f32[2048]{0:T(1024)S(1)} %rsqrt.25, f32[2048]{0:T(1024)S(1)} %div.52, f32[768]{0:T(1024)S(1)} %mul.622, bf16[3072,768]{1,0:T(8,128)(2,1)} %bitcast.163, ...), kind=kOutput, calls=%fused_computation.39 | convolution fusion | flops 9679400960 | bytes 36217856 | tf_op jit(solution)/shard_map/dot_general | solution.py:150
  414.7 6.5 all-to-all-start.1
  421.2 7.2 %fusion.68 = (f32[2048]{0:T(1024)S(1)}, f32[2048,768]{1,0:T(8,128)S(1)}, bf16[2048,768]{1,0:T(8,128)(2,1)}) fusion(f32[2048]{0:T(1024)S(1)} %multiply_multiply_fusion.2, f32[2048]{0:T(1024)S(1)} %div.52, f32[32,64,768]{2,1,0:T(8,128)} %get-tuple-element.81, f32[2048]{0:T(1024)S(1)} %rsqrt.25, f32[2048,768]{1,0:T(8,128)} %get-tuple-element.86, ...), kind=kLoop, calls=%fused_computation.193 | loop fusion | flops 17299456 | bytes 22059008 | tf_op jit(solution)/shard_map/transpose(jvp())/reduce_sum | solution.py:18
  428.4 14.2 %fusion.17 = f32[3072,768]{1,0:T(8,128)S(1)} fusion(bf16[2048,768]{1,0:T(8,128)(2,1)} %get-tuple-element.70, bf16[2048,3072]{1,0:T(8,128)(2,1)} %get-tuple-element.88), kind=kOutput, calls=%fused_computation.43 | convolution fusion | flops 9663676416 | bytes 25165824 | tf_op jit(solution)/shard_map/tf,td->fd/dot_general | solution.py:149
  448.9 8.9 %convert_bitcast_fusion.1 = bf16[32,2,64,768]{3,2,0,1:T(8,128)(2,1)} fusion(bf16[32,64,768,1]{2,1,0,3:T(8,128)(2,1)} %bitcast.167, bf16[1,768,768]{2,1,0:T(8,128)(2,1)S(1)} %copy-done.11, bf16[1,768,768]{2,1,0:T(8,128)(2,1)} %multiply_convert_fusion.2), kind=kOutput, calls=%fused_computation.40 | convolution fusion | flops 4839702528 | bytes 11796480 | tf_op jit(solution)/shard_map/lne,ude->lund/dot_general | solution.py:154
  486.4 9.8 %all-to-all-start.3 = ((bf16[16,2,64,768]{3,1,2,0:T(2,128)(2,1)}), bf16[16,2,64,768]{3,1,2,0:T(2,128)(2,1)}, u32[]{:S(2)}, u32[]{:S(2)}) async-start(bf16[16,2,64,768]{3,1,2,0:T(2,128)(2,1)} %copy.60), calls=%async_computation.3 | async-start | bytes 6291456 | tf_op jit(solution)/shard_map/all_to_all | solution.py:168
  508.4 19.3 %collective-permute-done.11 = bf16[8,96,768]{2,1,0:T(8,128)(2,1)} collective-permute-done((bf16[8,96,768]{2,1,0:T(8,128)(2,1)}, bf16[8,96,768]{2,1,0:T(8,128)(2,1)}, u32[]{:S(2)}, u32[]{:S(2)}) %collective-permute-start.11) | collective-permute-done | bytes 1179680 | tf_op jit(solution)/shard_map/ppermute | solution.py:49
  532.2 5.6 collective-permute-done.17
  538.7 19.7 %collective-permute-done.12 = bf16[4,96,768]{2,1,0:T(8,128)(2,1)S(1)} collective-permute-done((bf16[4,96,768]{2,1,0:T(8,128)(2,1)S(1)}, bf16[4,96,768]{2,1,0:T(8,128)(2,1)S(1)}, u32[]{:S(2)}, u32[]{:S(2)}) %collective-permute-start.12) | collective-permute-done | bytes 589856 | tf_op jit(solution)/shard_map/ppermute | solution.py:49
  561.3 7.2 %collective-permute-done.13 = bf16[2,96,768]{2,1,0:T(8,128)(2,1)} collective-permute-done((bf16[2,96,768]{2,1,0:T(8,128)(2,1)}, bf16[2,96,768]{2,1,0:T(8,128)(2,1)}, u32[]{:S(2)}, u32[]{:S(2)}) %collective-permute-start.13) | collective-permute-done | bytes 294944 | tf_op jit(solution)/shard_map/ppermute | solution.py:49
  569.7 8.5 %collective-permute-start.14 = (bf16[1,96,768]{2,1,0:T(8,128)(2,1)S(1)}, bf16[1,96,768]{2,1,0:T(8,128)(2,1)S(1)}, u32[]{:S(2)}, u32[]{:S(2)}) collective-permute-start(bf16[1,96,768]{2,1,0:T(8,128)(2,1)S(1)} %slice.266), channel_id=1, source_target_pairs={{0,8},{1,9},{2,10},{3,11},{4,12},{5,13},{6,14},{7,15},{8,0},{9,1},... | collective-permute-start | bytes 442376 | tf_op jit(solution)/shard_map/ppermute | solution.py:49
  579.0 6.4 collective-permute-done.14
  588.7 13.2 %fusion.22 = (f32[16,2,64]{1,2,0:T(8,128)S(1)}, f32[16,2,64]{1,2,0:T(8,128)S(1)}) fusion(bf16[16,2,64,768]{3,1,2,0:T(2,128)(2,1)S(1)} %all-to-all-done.1, f32[16,2,64]{1,2,0:T(8,128)S(1)} %reduce_max.15, s32[16,2,64]{1,2,0:T(8,128)} %copy.62), kind=kLoop, calls=%fused_computation.60 | loop fusion | flops 9433088 | bytes 3178496 | tf_op jit(solution)/shard_map/reduce_sum | solution.py:195
  604.3 57.7 %psum.14 = f32[10,768]{1,0:T(8,128)S(1)} all-reduce(f32[10,768]{1,0:T(8,128)S(1)} %concatenate.64), channel_id=1, replica_groups=mesh['batch'=2,'seq'=16] {'seq'}, use_global_device_ids=true, to_apply=%region_20.21 | all-reduce | flops 7680 | bytes 61440 | tf_op jit(solution)/shard_map/psum | solution.py:211
  662.0 7.9 %psum.15 = f32[10,768]{1,0:T(8,128)S(1)} all-reduce(f32[10,768]{1,0:T(8,128)S(1)} %psum.14), channel_id=1, replica_groups=mesh['batch'=2,'seq'=16] {'batch'}, use_global_device_ids=true, to_apply=%region_21.22 | all-reduce | flops 7680 | bytes 61440 | tf_op jit(solution)/shard_map/psum | solution.py:211
  675.4 5.9 copy.77
  (265 shorter events, 144.0 us)
Async XLA Ops:
  0.6 45.3 %copy-start.36 = (s32[32]{0:T(128)S(1)}, s32[32]{0:T(128)}, u32[]{:S(2)}) copy-start(s32[32]{0:T(128)} %constant.129.clone) | copy-start | bytes 388
  0.7 42.8 %copy-start.34 = (bf16[1,3,24]{2,1,0:T(4,128)(2,1)S(1)}, bf16[1,3,24]{2,1,0:T(4,128)(2,1)}, u32[]{:S(2)}) copy-start(bf16[1,3,24]{2,1,0:T(4,128)(2,1)} %param.19) | copy-start | bytes 436
  0.7 42.9 %copy-start.35 = (bf16[1,2,24]{2,1,0:T(2,128)(2,1)S(1)}, bf16[1,2,24]{2,1,0:T(2,128)(2,1)}, u32[]{:S(2)}) copy-start(bf16[1,2,24]{2,1,0:T(2,128)(2,1)} %param.20) | copy-start | bytes 292
  0.7 42.9 %copy-start.32 = (s32[16]{0:T(128)S(1)}, s32[16]{0:T(128)}, u32[]{:S(2)}) copy-start(s32[16]{0:T(128)} %param.12) | copy-start | bytes 196
  1.7 17.4 %collective-permute-start = (bf16[1,2,96,768]{3,2,1,0:T(8,128)(2,1)S(1)}, bf16[1,2,96,768]{3,2,1,0:T(8,128)(2,1)S(1)}, u32[]{:S(2)}, u32[]{:S(2)}) collective-permute-start(bf16[1,2,96,768]{3,2,1,0:T(8,128)(2,1)S(1)} %maximum_bitcast_fusion.1), channel_id=1, source_target_pairs={{0,8},{1,9},{2,10},{3,11},{4,12},{5,13},{6,14},{7,15},{8,0},{9,1},... | collective-permute-start | bytes 884744 | tf_op jit(solution)/shard_map/ppermute | solution.py:49
  19.2 14.6 %collective-permute-start.1 = (bf16[2,2,96,768]{3,2,1,0:T(8,128)(2,1)S(1)}, bf16[2,2,96,768]{3,2,1,0:T(8,128)(2,1)S(1)}, u32[]{:S(2)}, u32[]{:S(2)}) collective-permute-start(bf16[2,2,96,768]{3,2,1,0:T(8,128)(2,1)S(1)} %pad_maximum_fusion.6), channel_id=1, source_target_pairs={{0,4},{1,5},{2,6},{3,7},{4,0},{5,1},{6,2},{7,3},{8,12},{9,13},{10,... | collective-permute-start | bytes 1769480 | tf_op jit(solution)/shard_map/ppermute | solution.py:49
  33.9 185.7 %copy-start.28 = (s32[16,64,2]{1,2,0:T(2,128)S(1)}, s32[16,64,2]{1,2,0:T(2,128)}, u32[]{:S(2)}) copy-start(s32[16,64,2]{1,2,0:T(2,128)} %param.14) | copy-start | bytes 24580
  33.9 196.9 %all-to-all-start = ((bf16[16,64,2,768]{3,2,1,0:T(2,128)(2,1)}), bf16[16,64,2,768]{3,2,1,0:T(2,128)(2,1)}, u32[]{:S(2)}, u32[]{:S(2)}) async-start(bf16[16,64,2,768]{3,2,1,0:T(2,128)(2,1)} %param.11), calls=%async_computation | async-start | bytes 6291456 | tf_op jit(solution)/shard_map/all_to_all | solution.py:112
  40.6 160.3 %collective-permute-start.5 = (f32[1,96]{1,0:T(1,128)S(1)}, f32[1,96]{1,0:T(1,128)S(1)}, u32[]{:S(2)}, u32[]{:S(2)}) collective-permute-start(f32[1,96]{1,0:T(1,128)S(1)} %convert_element_type.301), channel_id=1, source_target_pairs={{0,8},{1,9},{2,10},{3,11},{4,12},{5,13},{6,14},{7,15},{8,0},{9,1},... | collective-permute-start | bytes 1160 | tf_op jit(solution)/shard_map/ppermute | solution.py:49
  44.2 58.4 %collective-permute-start.2 = (bf16[4,2,96,768]{3,2,1,0:T(8,128)(2,1)S(1)}, bf16[4,2,96,768]{3,2,1,0:T(8,128)(2,1)S(1)}, u32[]{:S(2)}, u32[]{:S(2)}) collective-permute-start(bf16[4,2,96,768]{3,2,1,0:T(8,128)(2,1)S(1)} %pad_maximum_fusion.5), channel_id=1, source_target_pairs={{0,2},{1,3},{2,0},{3,1},{4,6},{5,7},{6,4},{7,5},{8,10},{9,11},{10,... | collective-permute-start | bytes 3538952 | tf_op jit(solution)/shard_map/ppermute | solution.py:49
  46.6 194.3 %copy-start.29 = (pred[32,64]{1,0:T(8,128)(4,1)}, pred[32,64]{1,0:T(8,128)(4,1)S(1)}, u32[]{:S(2)}) copy-start(pred[32,64]{1,0:T(8,128)(4,1)S(1)} %add_compare_fusion) | copy-start | bytes 6148
  104.3 119.2 %collective-permute-start.3 = (bf16[8,2,96,768]{3,2,1,0:T(8,128)(2,1)}, bf16[8,2,96,768]{3,2,1,0:T(8,128)(2,1)}, u32[]{:S(2)}, u32[]{:S(2)}) collective-permute-start(bf16[8,2,96,768]{3,2,1,0:T(8,128)(2,1)} %pad_maximum_fusion.2), channel_id=1, source_target_pairs={{0,16},{16,0},{1,17},{17,1},{2,18},{18,2},{3,19},{19,3},{4,20},{20... | collective-permute-start | bytes 7077896 | tf_op jit(solution)/shard_map/ppermute | solution.py:49
  200.9 10.0 %collective-permute-start.6 = (f32[2,96]{1,0:T(2,128)S(1)}, f32[2,96]{1,0:T(2,128)S(1)}, u32[]{:S(2)}, u32[]{:S(2)}) collective-permute-start(f32[2,96]{1,0:T(2,128)S(1)} %pad_maximum_fusion.10), channel_id=1, source_target_pairs={{0,4},{1,5},{2,6},{3,7},{4,0},{5,1},{6,2},{7,3},{8,12},{9,13},{10,... | collective-permute-start | bytes 2312 | tf_op jit(solution)/shard_map/ppermute | solution.py:49
  210.9 3.9 collective-permute-start.7
  214.8 3.7 collective-permute-start.8
  218.5 2.6 collective-permute-start.9
  227.1 41.2 %collective-permute-start.4 = (bf16[16,2,96,768]{3,2,1,0:T(8,128)(2,1)}, bf16[16,2,96,768]{3,2,1,0:T(8,128)(2,1)}, u32[]{:S(2)}, u32[]{:S(2)}) collective-permute-start(bf16[16,2,96,768]{3,2,1,0:T(8,128)(2,1)} %pad_maximum_fusion), channel_id=1, source_target_pairs={{0,1},{1,0},{2,3},{3,2},{4,5},{5,4},{6,7},{7,6},{8,9},{9,8},{10,11... | collective-permute-start | bytes 14155784 | tf_op jit(solution)/shard_map/ppermute | solution.py:49
  235.1 90.9 %all-to-all-start.2 = ((bf16[16,64,2,768]{3,2,1,0:T(2,128)(2,1)}), bf16[16,64,2,768]{3,2,1,0:T(2,128)(2,1)S(1)}, u32[]{:S(2)}, u32[]{:S(2)}) async-start(bf16[16,64,2,768]{3,2,1,0:T(2,128)(2,1)} %param.15), calls=%async_computation.2 | async-start | bytes 6291456 | tf_op jit(solution)/shard_map/all_to_all | solution.py:114
  338.3 59.0 %copy-start.2 = (f32[2048,768]{1,0:T(8,128)}, f32[2048,768]{1,0:T(8,128)S(1)}, u32[]{:S(2)}) copy-start(f32[2048,768]{1,0:T(8,128)S(1)} %get-tuple-element.63) | copy-start | bytes 18874372
  356.1 41.2 %slice-start.3 = ((s8[6291456]{0:T(1024)(128)(4,1)}), s8[2097152]{0:T(1024)(128)(4,1)S(1)}, s32[]{:S(2)}) async-start(s8[6291456]{0:T(1024)(128)(4,1)} %bitcast.143), calls=%async_computation.7 | async-start | bytes 4194304
  414.7 71.7 %all-to-all-start.1 = ((bf16[16,2,64,768]{3,1,2,0:T(2,128)(2,1)}), bf16[16,2,64,768]{3,1,2,0:T(2,128)(2,1)S(1)}, u32[]{:S(2)}, u32[]{:S(2)}) async-start(bf16[16,2,64,768]{3,1,2,0:T(2,128)(2,1)} %copy.55), calls=%async_computation.1 | async-start | bytes 6291456 | tf_op jit(solution)/shard_map/all_to_all | solution.py:136
  446.1 23.5 %collective-permute-start.15 = (bf16[16,96,768]{2,1,0:T(8,128)(2,1)}, bf16[16,96,768]{2,1,0:T(8,128)(2,1)}, u32[]{:S(2)}, u32[]{:S(2)}) collective-permute-start(bf16[16,96,768]{2,1,0:T(8,128)(2,1)} %bitcast.57), channel_id=1, source_target_pairs={{0,1},{1,0},{2,3},{3,2},{4,5},{5,4},{6,7},{7,6},{8,9},{9,8},{10,11... | collective-permute-start | bytes 7077896 | tf_op jit(solution)/shard_map/ppermute | solution.py:49
  446.6 27.7 %collective-permute-start.10 = (bf16[16,96,768]{2,1,0:T(8,128)(2,1)}, bf16[16,96,768]{2,1,0:T(8,128)(2,1)}, u32[]{:S(2)}, u32[]{:S(2)}) collective-permute-start(bf16[16,96,768]{2,1,0:T(8,128)(2,1)} %bitcast.47), channel_id=1, source_target_pairs={{0,1},{1,0},{2,3},{3,2},{4,5},{5,4},{6,7},{7,6},{8,9},{9,8},{10,11... | collective-permute-start | bytes 7077896 | tf_op jit(solution)/shard_map/ppermute | solution.py:49
  473.7 30.2 %collective-permute-start.16 = (bf16[8,96,768]{2,1,0:T(8,128)(2,1)}, bf16[8,96,768]{2,1,0:T(8,128)(2,1)}, u32[]{:S(2)}, u32[]{:S(2)}) collective-permute-start(bf16[8,96,768]{2,1,0:T(8,128)(2,1)} %slice.259), channel_id=1, source_target_pairs={{0,16},{16,0},{1,17},{17,1},{2,18},{18,2},{3,19},{19,3},{4,20},{20... | collective-permute-start | bytes 3538952 | tf_op jit(solution)/shard_map/ppermute | solution.py:49
  478.2 49.5 %collective-permute-start.11 = (bf16[8,96,768]{2,1,0:T(8,128)(2,1)}, bf16[8,96,768]{2,1,0:T(8,128)(2,1)}, u32[]{:S(2)}, u32[]{:S(2)}) collective-permute-start(bf16[8,96,768]{2,1,0:T(8,128)(2,1)} %slice.260), channel_id=1, source_target_pairs={{0,16},{16,0},{1,17},{17,1},{2,18},{18,2},{3,19},{19,3},{4,20},{20... | collective-permute-start | bytes 3538952 | tf_op jit(solution)/shard_map/ppermute | solution.py:49
  486.4 185.4 %all-to-all-start.3 = ((bf16[16,2,64,768]{3,1,2,0:T(2,128)(2,1)}), bf16[16,2,64,768]{3,1,2,0:T(2,128)(2,1)}, u32[]{:S(2)}, u32[]{:S(2)}) async-start(bf16[16,2,64,768]{3,1,2,0:T(2,128)(2,1)} %copy.60), calls=%async_computation.3 | async-start | bytes 6291456 | tf_op jit(solution)/shard_map/all_to_all | solution.py:168
  506.3 31.5 %collective-permute-start.17 = (bf16[4,96,768]{2,1,0:T(8,128)(2,1)S(1)}, bf16[4,96,768]{2,1,0:T(8,128)(2,1)S(1)}, u32[]{:S(2)}, u32[]{:S(2)}) collective-permute-start(bf16[4,96,768]{2,1,0:T(8,128)(2,1)S(1)} %slice.261), channel_id=1, source_target_pairs={{0,2},{1,3},{2,0},{3,1},{4,6},{5,7},{6,4},{7,5},{8,10},{9,11},{10,... | collective-permute-start | bytes 1769480 | tf_op jit(solution)/shard_map/ppermute | solution.py:49
  529.9 28.4 %collective-permute-start.12 = (bf16[4,96,768]{2,1,0:T(8,128)(2,1)S(1)}, bf16[4,96,768]{2,1,0:T(8,128)(2,1)S(1)}, u32[]{:S(2)}, u32[]{:S(2)}) collective-permute-start(bf16[4,96,768]{2,1,0:T(8,128)(2,1)S(1)} %slice.262), channel_id=1, source_target_pairs={{0,2},{1,3},{2,0},{3,1},{4,6},{5,7},{6,4},{7,5},{8,10},{9,11},{10,... | collective-permute-start | bytes 1769480 | tf_op jit(solution)/shard_map/ppermute | solution.py:49
  538.7 21.3 %collective-permute-start.18 = (bf16[2,96,768]{2,1,0:T(8,128)(2,1)}, bf16[2,96,768]{2,1,0:T(8,128)(2,1)}, u32[]{:S(2)}, u32[]{:S(2)}) collective-permute-start(bf16[2,96,768]{2,1,0:T(8,128)(2,1)} %slice.263), channel_id=1, source_target_pairs={{0,4},{1,5},{2,6},{3,7},{4,0},{5,1},{6,2},{7,3},{8,12},{9,13},{10,... | collective-permute-start | bytes 884744 | tf_op jit(solution)/shard_map/ppermute | solution.py:49
  559.6 8.9 %collective-permute-start.13 = (bf16[2,96,768]{2,1,0:T(8,128)(2,1)}, bf16[2,96,768]{2,1,0:T(8,128)(2,1)}, u32[]{:S(2)}, u32[]{:S(2)}) collective-permute-start(bf16[2,96,768]{2,1,0:T(8,128)(2,1)} %slice.264), channel_id=1, source_target_pairs={{0,4},{1,5},{2,6},{3,7},{4,0},{5,1},{6,2},{7,3},{8,12},{9,13},{10,... | collective-permute-start | bytes 884744 | tf_op jit(solution)/shard_map/ppermute | solution.py:49
  561.2 17.0 %collective-permute-start.19 = (bf16[1,96,768]{2,1,0:T(8,128)(2,1)S(1)}, bf16[1,96,768]{2,1,0:T(8,128)(2,1)S(1)}, u32[]{:S(2)}, u32[]{:S(2)}) collective-permute-start(bf16[1,96,768]{2,1,0:T(8,128)(2,1)S(1)} %slice.265), channel_id=1, source_target_pairs={{0,8},{1,9},{2,10},{3,11},{4,12},{5,13},{6,14},{7,15},{8,0},{9,1},... | collective-permute-start | bytes 442376 | tf_op jit(solution)/shard_map/ppermute | solution.py:49
  569.7 15.6 %collective-permute-start.14 = (bf16[1,96,768]{2,1,0:T(8,128)(2,1)S(1)}, bf16[1,96,768]{2,1,0:T(8,128)(2,1)S(1)}, u32[]{:S(2)}, u32[]{:S(2)}) collective-permute-start(bf16[1,96,768]{2,1,0:T(8,128)(2,1)S(1)} %slice.266), channel_id=1, source_target_pairs={{0,8},{1,9},{2,10},{3,11},{4,12},{5,13},{6,14},{7,15},{8,0},{9,1},... | collective-permute-start | bytes 442376 | tf_op jit(solution)/shard_map/ppermute | solution.py:49
  (40 other events, 546.6 us)
